TPU v7x, 32 devices: a whole 2x2x4 slice. The times are simulated.
32 devices in a mesh: strip: 8 (over z, x), wave: 4 (over y, core).
Axes of the slice: x: 2, y: 2, z: 4, core: 2. Of those that a mesh axis runs over, the one named last changes fastest.
Arguments:
- source: bfloat16 [16, 1024, 2, 512], P('strip', None, None, 'wave'), parts along dimension 3, may hold values from -4 to 4
- pivot_inverse_real: bfloat16 [16, 4096, 1024], P('strip', 'wave'), parts along dimension 1, may hold values from -1 to 1
- factor_imag: bfloat16 [16, 4096, 1024], P('strip', 'wave'), parts along dimension 1, may hold values from -1 to 1
Outputs:
- solution: bfloat16 [16, 1024, 2, 512], P('strip', None, None, 'wave'), parts along dimension 3
There are 4 independent parts, one for each index of `wave`. A program takes and returns all parts, laid end to end along the dimension named above; each array names one. Nothing has to cross between parts.
All inputs are finite; a program needn't handle non-finite values.
Results may differ from a plain program's by a relative error of at most 0.033.
Values may be sent and summed in bfloat16 or wider, within the bound.
A program may use at most 64 MiB of HBM per device.

v0:
```python
import jax
import jax.numpy as jnp
from jax import lax
from jax.sharding import PartitionSpec as P

MICRO = 64


def shifted(value, axis, steps):
    count = lax.axis_size(axis)
    initial, last = (max(0, -steps), min(count, count - steps))
    return lax.ppermute(value, axis, [(source, source + steps) for source in range(initial, last)])


def complex_apply(real_part, imag_part, vector):
    mode_count, halves, columns = vector.shape
    merged = vector.reshape(mode_count, halves * columns)
    direct = jnp.dot(real_part, merged, preferred_element_type=jnp.float32).reshape(
        mode_count, halves, columns
    )
    crossed = jnp.dot(imag_part, merged, preferred_element_type=jnp.float32).reshape(
        mode_count, halves, columns
    )
    return jnp.stack([direct[:, 0] - crossed[:, 1], direct[:, 1] + crossed[:, 0]], axis=1)


def forward_block(block_source, pivot_inverse_real, factor_imag, incoming):
    traces = []
    trace_now = incoming
    for layer_index in range(block_source.shape[0]):
        summed = (block_source[layer_index].astype(jnp.float32) + trace_now).astype(jnp.bfloat16)
        trace_now = complex_apply(pivot_inverse_real[layer_index], factor_imag[layer_index], summed)
        traces.append(trace_now)
    return (jnp.stack(traces), trace_now)


def backward_block(block_traces, pivot_inverse_real, factor_imag, incoming):
    layer_count = block_traces.shape[0]
    fields = [None] * layer_count
    field_now = incoming
    for layer_index in reversed(range(layer_count)):
        field_now = block_traces[layer_index] + complex_apply(
            pivot_inverse_real[layer_index],
            factor_imag[layer_index],
            field_now.astype(jnp.bfloat16),
        )
        fields[layer_index] = field_now
    return (jnp.stack(fields), field_now.astype(jnp.bfloat16))


def shards(source, pivot_inverse_real, factor_imag):
    strips = lax.axis_size("strip")
    position = lax.axis_index("strip")
    layer_count, mode_count, halves, sources = source.shape
    block_size = MICRO
    batches = sources // block_size
    empty = jnp.zeros((mode_count, halves, block_size), jnp.float32)
    empty_half = jnp.zeros((mode_count, halves, block_size), jnp.bfloat16)

    def advance(moment, state, back_start, do_forward, do_backward):
        down_send, up_send, traces, fields = state
        if do_forward:
            received = shifted(down_send, "strip", 1)
            which = moment - position
            active = jnp.logical_and(which >= 0, which < batches)
            offset = jnp.clip(which, 0, batches - 1) * block_size

            def compute_forward(current):
                block_source = lax.dynamic_slice_in_dim(source, offset, block_size, 3)
                new_traces, last_trace = forward_block(
                    block_source, pivot_inverse_real, factor_imag, received
                )
                return (lax.dynamic_update_slice_in_dim(current, new_traces, offset, 3), last_trace)

            def remain_forward(current):
                return (current, down_send)

            traces, down_send = lax.cond(active, compute_forward, remain_forward, traces)
        if do_backward:
            arrived = shifted(up_send, "strip", -1)
            which = moment - back_start - (strips - 1 - position)
            active = jnp.logical_and(which >= 0, which < batches)
            offset = jnp.clip(which, 0, batches - 1) * block_size

            def evaluate_backward_sweep(current):
                block_traces = lax.dynamic_slice_in_dim(traces, offset, block_size, 3)
                new_fields, first_field = backward_block(
                    block_traces, pivot_inverse_real, factor_imag, arrived
                )
                return (
                    lax.dynamic_update_slice_in_dim(
                        current, new_fields.astype(jnp.bfloat16), offset, 3
                    ),
                    first_field,
                )

            def remain_backward(current):
                return (current, up_send)

            fields, up_send = lax.cond(active, evaluate_backward_sweep, remain_backward, fields)
        return (down_send, up_send, traces, fields)

    state = (
        empty,
        empty_half,
        jnp.zeros(source.shape, jnp.float32),
        jnp.zeros(source.shape, jnp.bfloat16),
    )
    state = lax.fori_loop(
        0,
        strips + batches - 1,
        lambda moment, current: advance(moment, current, 0, True, False),
        state,
    )
    state = lax.fori_loop(
        0,
        strips + batches - 1,
        lambda moment, current: advance(moment, current, 0, False, True),
        state,
    )
    return state[3]


def solution(mesh):
    placed = (P("strip", None, None, "wave"), P("strip", "wave", None), P("strip", "wave", None))
    return jax.shard_map(
        shards,
        mesh=mesh,
        in_specs=placed,
        out_specs=P("strip", None, None, "wave"),
        check_vma=False,
    )
```

profile of v0, /device:TPU:0, one launch (start us, length us, event | category | flops | bytes accessed | tf_op | source)
XLA Modules:
  0.0 374.1 jit_solution(3431112014103794212)
XLA Ops:
  0.0 3.7 copy.4
  4.0 166.4 %while.32 = (s32[]{:T(128)}, f32[1024,2,64]{0,2,1:T(8,128)S(1)}, f32[2,1024,2,128]{1,3,2,0:T(8,128)S(1)}, s32[]{:T(128)}, bf16[2,1024,2,128]{1,3,2,0:T(8,128)(2,...) while((s32[]{:T(128)}, f32[1024,2,64]{0,2,1:T(8,128)S(1)}, ...), condition=%wide.region_3.4_spmd, body=%wide.region_0.3_spmd.sunk | while | flops 1075445760 | bytes 40370568 | solution.py:109
  4.0 4.9 %collective-permute-start = (f32[1024,2,64]{0,2,1:T(8,128)S(1)}, f32[1024,2,64]{0,2,1:T(8,128)S(1)}, u32[]{:S(2)}, u32[]{:S(2)}) collective-permute-start(f32[1024,2,64]{0,2,1:T(8,128)S(1)} %get-tuple-element.565), channel_id=1, source_target_pairs={{0,4},{4,8},{8,12},{12,16},{16,20},{20,24},{24,28},{1,5},{5,9},{9,... | collective-permute-start | bytes 1572872 | tf_op jit(solution)/shard_map/while/body/eval_jaxpr/ppermute | solution.py:12
  8.9 11.1 %collective-permute-done = f32[1024,2,64]{0,2,1:T(8,128)S(1)} collective-permute-done((f32[1024,2,64]{0,2,1:T(8,128)S(1)}, f32[1024,2,64]{0,2,1:T(8,128)S(1)}, u32[]{:S(2)}, u32[]{:S(2)}) %collective-permute-start) | collective-permute-done | bytes 524320 | tf_op jit(solution)/shard_map/while/body/eval_jaxpr/ppermute | solution.py:12
  20.0 10.8 %conditional.4 = ((f32[2,1024,2,128]{1,3,2,0:T(8,128)S(1)}, f32[1024,2,64]{0,2,1:T(8,128)S(1)})) conditional(s32[]{:T(128)} %convert_element_type.87, (f32[2,1024,2,128]{1,3,2,0:T(8,128)S(1)}, f32[1024,2,64]{0,2,1:T(8,128)S(1)}) %tuple.91, (s32[]{:T(128)}, bf16[2,1024,2,128]{1,3,2,0:T(8,128)(2,1)}, f32[1024,2,64]{0,2,1:T(8,128)S(1)}, ...), branch_computations={%region_1.1_spmd, %region_2.2_spmd} | conditional | flops 1075445760 | bytes 38273172 | solution.py:78
  21.0 2.4 fusion.6
  23.5 2.4 fusion.4
  27.1 2.6 fusion.2
  30.9 1.3 collective-permute-start
  32.2 10.5 %collective-permute-done = f32[1024,2,64]{0,2,1:T(8,128)S(1)} collective-permute-done((f32[1024,2,64]{0,2,1:T(8,128)S(1)}, f32[1024,2,64]{0,2,1:T(8,128)S(1)}, u32[]{:S(2)}, u32[]{:S(2)}) %collective-permute-start) | collective-permute-done | bytes 524320 | tf_op jit(solution)/shard_map/while/body/eval_jaxpr/ppermute | solution.py:12
  42.8 10.8 %conditional.4 = ((f32[2,1024,2,128]{1,3,2,0:T(8,128)S(1)}, f32[1024,2,64]{0,2,1:T(8,128)S(1)})) conditional(s32[]{:T(128)} %convert_element_type.87, (f32[2,1024,2,128]{1,3,2,0:T(8,128)S(1)}, f32[1024,2,64]{0,2,1:T(8,128)S(1)}) %tuple.91, (s32[]{:T(128)}, bf16[2,1024,2,128]{1,3,2,0:T(8,128)(2,1)}, f32[1024,2,64]{0,2,1:T(8,128)S(1)}, ...), branch_computations={%region_1.1_spmd, %region_2.2_spmd} | conditional | flops 1075445760 | bytes 38273172 | solution.py:78
  43.8 2.4 fusion.6
  46.2 2.4 fusion.4
  49.9 2.6 fusion.2
  53.6 4.4 %collective-permute-start = (f32[1024,2,64]{0,2,1:T(8,128)S(1)}, f32[1024,2,64]{0,2,1:T(8,128)S(1)}, u32[]{:S(2)}, u32[]{:S(2)}) collective-permute-start(f32[1024,2,64]{0,2,1:T(8,128)S(1)} %get-tuple-element.565), channel_id=1, source_target_pairs={{0,4},{4,8},{8,12},{12,16},{16,20},{20,24},{24,28},{1,5},{5,9},{9,... | collective-permute-start | bytes 1572872 | tf_op jit(solution)/shard_map/while/body/eval_jaxpr/ppermute | solution.py:12
  58.1 9.7 %collective-permute-done = f32[1024,2,64]{0,2,1:T(8,128)S(1)} collective-permute-done((f32[1024,2,64]{0,2,1:T(8,128)S(1)}, f32[1024,2,64]{0,2,1:T(8,128)S(1)}, u32[]{:S(2)}, u32[]{:S(2)}) %collective-permute-start) | collective-permute-done | bytes 524320 | tf_op jit(solution)/shard_map/while/body/eval_jaxpr/ppermute | solution.py:12
  67.8 15.3 %collective-permute-start = (f32[1024,2,64]{0,2,1:T(8,128)S(1)}, f32[1024,2,64]{0,2,1:T(8,128)S(1)}, u32[]{:S(2)}, u32[]{:S(2)}) collective-permute-start(f32[1024,2,64]{0,2,1:T(8,128)S(1)} %get-tuple-element.565), channel_id=1, source_target_pairs={{0,4},{4,8},{8,12},{12,16},{16,20},{20,24},{24,28},{1,5},{5,9},{9,... | collective-permute-start | bytes 1572872 | tf_op jit(solution)/shard_map/while/body/eval_jaxpr/ppermute | solution.py:12
  83.1 8.8 %collective-permute-done = f32[1024,2,64]{0,2,1:T(8,128)S(1)} collective-permute-done((f32[1024,2,64]{0,2,1:T(8,128)S(1)}, f32[1024,2,64]{0,2,1:T(8,128)S(1)}, u32[]{:S(2)}, u32[]{:S(2)}) %collective-permute-start) | collective-permute-done | bytes 524320 | tf_op jit(solution)/shard_map/while/body/eval_jaxpr/ppermute | solution.py:12
  91.9 4.4 %collective-permute-start = (f32[1024,2,64]{0,2,1:T(8,128)S(1)}, f32[1024,2,64]{0,2,1:T(8,128)S(1)}, u32[]{:S(2)}, u32[]{:S(2)}) collective-permute-start(f32[1024,2,64]{0,2,1:T(8,128)S(1)} %get-tuple-element.565), channel_id=1, source_target_pairs={{0,4},{4,8},{8,12},{12,16},{16,20},{20,24},{24,28},{1,5},{5,9},{9,... | collective-permute-start | bytes 1572872 | tf_op jit(solution)/shard_map/while/body/eval_jaxpr/ppermute | solution.py:12
  96.3 8.0 %collective-permute-done = f32[1024,2,64]{0,2,1:T(8,128)S(1)} collective-permute-done((f32[1024,2,64]{0,2,1:T(8,128)S(1)}, f32[1024,2,64]{0,2,1:T(8,128)S(1)}, u32[]{:S(2)}, u32[]{:S(2)}) %collective-permute-start) | collective-permute-done | bytes 524320 | tf_op jit(solution)/shard_map/while/body/eval_jaxpr/ppermute | solution.py:12
  104.3 15.4 %collective-permute-start = (f32[1024,2,64]{0,2,1:T(8,128)S(1)}, f32[1024,2,64]{0,2,1:T(8,128)S(1)}, u32[]{:S(2)}, u32[]{:S(2)}) collective-permute-start(f32[1024,2,64]{0,2,1:T(8,128)S(1)} %get-tuple-element.565), channel_id=1, source_target_pairs={{0,4},{4,8},{8,12},{12,16},{16,20},{20,24},{24,28},{1,5},{5,9},{9,... | collective-permute-start | bytes 1572872 | tf_op jit(solution)/shard_map/while/body/eval_jaxpr/ppermute | solution.py:12
  119.8 7.4 %collective-permute-done = f32[1024,2,64]{0,2,1:T(8,128)S(1)} collective-permute-done((f32[1024,2,64]{0,2,1:T(8,128)S(1)}, f32[1024,2,64]{0,2,1:T(8,128)S(1)}, u32[]{:S(2)}, u32[]{:S(2)}) %collective-permute-start) | collective-permute-done | bytes 524320 | tf_op jit(solution)/shard_map/while/body/eval_jaxpr/ppermute | solution.py:12
  127.1 5.3 %collective-permute-start = (f32[1024,2,64]{0,2,1:T(8,128)S(1)}, f32[1024,2,64]{0,2,1:T(8,128)S(1)}, u32[]{:S(2)}, u32[]{:S(2)}) collective-permute-start(f32[1024,2,64]{0,2,1:T(8,128)S(1)} %get-tuple-element.565), channel_id=1, source_target_pairs={{0,4},{4,8},{8,12},{12,16},{16,20},{20,24},{24,28},{1,5},{5,9},{9,... | collective-permute-start | bytes 1572872 | tf_op jit(solution)/shard_map/while/body/eval_jaxpr/ppermute | solution.py:12
  132.5 6.6 %collective-permute-done = f32[1024,2,64]{0,2,1:T(8,128)S(1)} collective-permute-done((f32[1024,2,64]{0,2,1:T(8,128)S(1)}, f32[1024,2,64]{0,2,1:T(8,128)S(1)}, u32[]{:S(2)}, u32[]{:S(2)}) %collective-permute-start) | collective-permute-done | bytes 524320 | tf_op jit(solution)/shard_map/while/body/eval_jaxpr/ppermute | solution.py:12
  139.1 12.7 %collective-permute-start = (f32[1024,2,64]{0,2,1:T(8,128)S(1)}, f32[1024,2,64]{0,2,1:T(8,128)S(1)}, u32[]{:S(2)}, u32[]{:S(2)}) collective-permute-start(f32[1024,2,64]{0,2,1:T(8,128)S(1)} %get-tuple-element.565), channel_id=1, source_target_pairs={{0,4},{4,8},{8,12},{12,16},{16,20},{20,24},{24,28},{1,5},{5,9},{9,... | collective-permute-start | bytes 1572872 | tf_op jit(solution)/shard_map/while/body/eval_jaxpr/ppermute | solution.py:12
  151.8 7.4 %collective-permute-done = f32[1024,2,64]{0,2,1:T(8,128)S(1)} collective-permute-done((f32[1024,2,64]{0,2,1:T(8,128)S(1)}, f32[1024,2,64]{0,2,1:T(8,128)S(1)}, u32[]{:S(2)}, u32[]{:S(2)}) %collective-permute-start) | collective-permute-done | bytes 524320 | tf_op jit(solution)/shard_map/while/body/eval_jaxpr/ppermute | solution.py:12
  159.2 4.5 %collective-permute-start = (f32[1024,2,64]{0,2,1:T(8,128)S(1)}, f32[1024,2,64]{0,2,1:T(8,128)S(1)}, u32[]{:S(2)}, u32[]{:S(2)}) collective-permute-start(f32[1024,2,64]{0,2,1:T(8,128)S(1)} %get-tuple-element.565), channel_id=1, source_target_pairs={{0,4},{4,8},{8,12},{12,16},{16,20},{20,24},{24,28},{1,5},{5,9},{9,... | collective-permute-start | bytes 1572872 | tf_op jit(solution)/shard_map/while/body/eval_jaxpr/ppermute | solution.py:12
  163.7 6.6 %collective-permute-done = f32[1024,2,64]{0,2,1:T(8,128)S(1)} collective-permute-done((f32[1024,2,64]{0,2,1:T(8,128)S(1)}, f32[1024,2,64]{0,2,1:T(8,128)S(1)}, u32[]{:S(2)}, u32[]{:S(2)}) %collective-permute-start) | collective-permute-done | bytes 524320 | tf_op jit(solution)/shard_map/while/body/eval_jaxpr/ppermute | solution.py:12
  171.5 198.9 %while.33 = (s32[]{:T(128)}, bf16[1024,2,64]{0,2,1:T(8,128)(2,1)S(1)}, bf16[2,1024,2,128]{1,3,2,0:T(8,128)(2,1)}, s32[]{:T(128)}, f32[2,1024,2,128]{1,3,2,0:T(8,...) while((s32[]{:T(128)}, ...), condition=%wide.region_7.8_spmd, body=%wide.region_4.7_spmd.sunk | while | flops 1076625408 | bytes 38797712 | solution.py:115
  171.5 1.3 collective-permute-start.1
  172.8 19.0 %collective-permute-done.1 = bf16[1024,2,64]{0,2,1:T(8,128)(2,1)S(1)} collective-permute-done((bf16[1024,2,64]{0,2,1:T(8,128)(2,1)S(1)}, bf16[1024,2,64]{0,2,1:T(8,128)(2,1)S(1)}, u32[]{:S(2)}, u32[]{:S(2)}) %collective-permute-start.1) | collective-permute-done | bytes 262176 | tf_op jit(solution)/shard_map/while/body/eval_jaxpr/ppermute | solution.py:12
  193.1 7.0 %collective-permute-done.1 = bf16[1024,2,64]{0,2,1:T(8,128)(2,1)S(1)} collective-permute-done((bf16[1024,2,64]{0,2,1:T(8,128)(2,1)S(1)}, bf16[1024,2,64]{0,2,1:T(8,128)(2,1)S(1)}, u32[]{:S(2)}, u32[]{:S(2)}) %collective-permute-start.1) | collective-permute-done | bytes 262176 | tf_op jit(solution)/shard_map/while/body/eval_jaxpr/ppermute | solution.py:12
  201.4 22.5 %collective-permute-done.1 = bf16[1024,2,64]{0,2,1:T(8,128)(2,1)S(1)} collective-permute-done((bf16[1024,2,64]{0,2,1:T(8,128)(2,1)S(1)}, bf16[1024,2,64]{0,2,1:T(8,128)(2,1)S(1)}, u32[]{:S(2)}, u32[]{:S(2)}) %collective-permute-start.1) | collective-permute-done | bytes 262176 | tf_op jit(solution)/shard_map/while/body/eval_jaxpr/ppermute | solution.py:12
  225.2 8.7 %collective-permute-done.1 = bf16[1024,2,64]{0,2,1:T(8,128)(2,1)S(1)} collective-permute-done((bf16[1024,2,64]{0,2,1:T(8,128)(2,1)S(1)}, bf16[1024,2,64]{0,2,1:T(8,128)(2,1)S(1)}, u32[]{:S(2)}, u32[]{:S(2)}) %collective-permute-start.1) | collective-permute-done | bytes 262176 | tf_op jit(solution)/shard_map/while/body/eval_jaxpr/ppermute | solution.py:12
  235.2 17.8 %collective-permute-done.1 = bf16[1024,2,64]{0,2,1:T(8,128)(2,1)S(1)} collective-permute-done((bf16[1024,2,64]{0,2,1:T(8,128)(2,1)S(1)}, bf16[1024,2,64]{0,2,1:T(8,128)(2,1)S(1)}, u32[]{:S(2)}, u32[]{:S(2)}) %collective-permute-start.1) | collective-permute-done | bytes 262176 | tf_op jit(solution)/shard_map/while/body/eval_jaxpr/ppermute | solution.py:12
  254.3 9.3 %collective-permute-done.1 = bf16[1024,2,64]{0,2,1:T(8,128)(2,1)S(1)} collective-permute-done((bf16[1024,2,64]{0,2,1:T(8,128)(2,1)S(1)}, bf16[1024,2,64]{0,2,1:T(8,128)(2,1)S(1)}, u32[]{:S(2)}, u32[]{:S(2)}) %collective-permute-start.1) | collective-permute-done | bytes 262176 | tf_op jit(solution)/shard_map/while/body/eval_jaxpr/ppermute | solution.py:12
  264.9 7.0 %collective-permute-done.1 = bf16[1024,2,64]{0,2,1:T(8,128)(2,1)S(1)} collective-permute-done((bf16[1024,2,64]{0,2,1:T(8,128)(2,1)S(1)}, bf16[1024,2,64]{0,2,1:T(8,128)(2,1)S(1)}, u32[]{:S(2)}, u32[]{:S(2)}) %collective-permute-start.1) | collective-permute-done | bytes 262176 | tf_op jit(solution)/shard_map/while/body/eval_jaxpr/ppermute | solution.py:12
  273.2 68.7 %collective-permute-done.1 = bf16[1024,2,64]{0,2,1:T(8,128)(2,1)S(1)} collective-permute-done((bf16[1024,2,64]{0,2,1:T(8,128)(2,1)S(1)}, bf16[1024,2,64]{0,2,1:T(8,128)(2,1)S(1)}, u32[]{:S(2)}, u32[]{:S(2)}) %collective-permute-start.1) | collective-permute-done | bytes 262176 | tf_op jit(solution)/shard_map/while/body/eval_jaxpr/ppermute | solution.py:12
  341.8 9.7 %conditional.5 = ((bf16[2,1024,2,128]{1,3,2,0:T(8,128)(2,1)}, bf16[1024,2,64]{0,2,1:T(8,128)(2,1)S(1)})) conditional(s32[]{:T(128)} %convert_element_type.88, (bf16[2,1024,2,128]{1,3,2,0:T(8,128)(2,1)}, bf16[1024,2,64]{0,2,1:T(8,128)(2,1)S(1)}) %tuple.94, (s32[]{:T(128)}, f32[2,1024,2,128]{1,3,2,0:T(8,128)S(1)}, bf16[2,1024,1024]{2,1,0:T(8,128)(2,1)}, ...), branch_computations={%region_5.5_spmd, %region_6.6_spmd} | conditional | flops 1076625408 | bytes 37748896 | solution.py:100
  341.8 2.4 fusion.19
  344.3 2.4 fusion.21
  346.8 2.6 fusion.17
  352.9 7.8 %collective-permute-done.1 = bf16[1024,2,64]{0,2,1:T(8,128)(2,1)S(1)} collective-permute-done((bf16[1024,2,64]{0,2,1:T(8,128)(2,1)S(1)}, bf16[1024,2,64]{0,2,1:T(8,128)(2,1)S(1)}, u32[]{:S(2)}, u32[]{:S(2)}) %collective-permute-start.1) | collective-permute-done | bytes 262176 | tf_op jit(solution)/shard_map/while/body/eval_jaxpr/ppermute | solution.py:12
  360.7 9.7 %conditional.5 = ((bf16[2,1024,2,128]{1,3,2,0:T(8,128)(2,1)}, bf16[1024,2,64]{0,2,1:T(8,128)(2,1)S(1)})) conditional(s32[]{:T(128)} %convert_element_type.88, (bf16[2,1024,2,128]{1,3,2,0:T(8,128)(2,1)}, bf16[1024,2,64]{0,2,1:T(8,128)(2,1)S(1)}) %tuple.94, (s32[]{:T(128)}, f32[2,1024,2,128]{1,3,2,0:T(8,128)S(1)}, bf16[2,1024,1024]{2,1,0:T(8,128)(2,1)}, ...), branch_computations={%region_5.5_spmd, %region_6.6_spmd} | conditional | flops 1076625408 | bytes 37748896 | solution.py:100
  360.7 2.4 fusion.19
  363.1 2.4 fusion.21
  365.7 2.6 fusion.17
  370.4 3.7 copy.5
  (64 shorter events, 22.8 us)
Async XLA Ops:
  4.0 16.0 %collective-permute-start = (f32[1024,2,64]{0,2,1:T(8,128)S(1)}, f32[1024,2,64]{0,2,1:T(8,128)S(1)}, u32[]{:S(2)}, u32[]{:S(2)}) collective-permute-start(f32[1024,2,64]{0,2,1:T(8,128)S(1)} %get-tuple-element.565), channel_id=1, source_target_pairs={{0,4},{4,8},{8,12},{12,16},{16,20},{20,24},{24,28},{1,5},{5,9},{9,... | collective-permute-start | bytes 1572872 | tf_op jit(solution)/shard_map/while/body/eval_jaxpr/ppermute | solution.py:12
  25.9 3.8 %copy-start = (bf16[2,1024,1024]{2,1,0:T(8,128)(2,1)S(1)}, bf16[2,1024,1024]{2,1,0:T(8,128)(2,1)}, u32[]{:S(2)}) copy-start(bf16[2,1024,1024]{2,1,0:T(8,128)(2,1)} %get-tuple-element.374) | copy-start | bytes 12582916 | tf_op jit(solution)/shard_map/while/body/eval_jaxpr/cond
  30.9 11.9 %collective-permute-start = (f32[1024,2,64]{0,2,1:T(8,128)S(1)}, f32[1024,2,64]{0,2,1:T(8,128)S(1)}, u32[]{:S(2)}, u32[]{:S(2)}) collective-permute-start(f32[1024,2,64]{0,2,1:T(8,128)S(1)} %get-tuple-element.565), channel_id=1, source_target_pairs={{0,4},{4,8},{8,12},{12,16},{16,20},{20,24},{24,28},{1,5},{5,9},{9,... | collective-permute-start | bytes 1572872 | tf_op jit(solution)/shard_map/while/body/eval_jaxpr/ppermute | solution.py:12
  48.7 3.8 %copy-start = (bf16[2,1024,1024]{2,1,0:T(8,128)(2,1)S(1)}, bf16[2,1024,1024]{2,1,0:T(8,128)(2,1)}, u32[]{:S(2)}) copy-start(bf16[2,1024,1024]{2,1,0:T(8,128)(2,1)} %get-tuple-element.374) | copy-start | bytes 12582916 | tf_op jit(solution)/shard_map/while/body/eval_jaxpr/cond
  53.6 14.1 %collective-permute-start = (f32[1024,2,64]{0,2,1:T(8,128)S(1)}, f32[1024,2,64]{0,2,1:T(8,128)S(1)}, u32[]{:S(2)}, u32[]{:S(2)}) collective-permute-start(f32[1024,2,64]{0,2,1:T(8,128)S(1)} %get-tuple-element.565), channel_id=1, source_target_pairs={{0,4},{4,8},{8,12},{12,16},{16,20},{20,24},{24,28},{1,5},{5,9},{9,... | collective-permute-start | bytes 1572872 | tf_op jit(solution)/shard_map/while/body/eval_jaxpr/ppermute | solution.py:12
  67.8 24.1 %collective-permute-start = (f32[1024,2,64]{0,2,1:T(8,128)S(1)}, f32[1024,2,64]{0,2,1:T(8,128)S(1)}, u32[]{:S(2)}, u32[]{:S(2)}) collective-permute-start(f32[1024,2,64]{0,2,1:T(8,128)S(1)} %get-tuple-element.565), channel_id=1, source_target_pairs={{0,4},{4,8},{8,12},{12,16},{16,20},{20,24},{24,28},{1,5},{5,9},{9,... | collective-permute-start | bytes 1572872 | tf_op jit(solution)/shard_map/while/body/eval_jaxpr/ppermute | solution.py:12
  91.9 12.4 %collective-permute-start = (f32[1024,2,64]{0,2,1:T(8,128)S(1)}, f32[1024,2,64]{0,2,1:T(8,128)S(1)}, u32[]{:S(2)}, u32[]{:S(2)}) collective-permute-start(f32[1024,2,64]{0,2,1:T(8,128)S(1)} %get-tuple-element.565), channel_id=1, source_target_pairs={{0,4},{4,8},{8,12},{12,16},{16,20},{20,24},{24,28},{1,5},{5,9},{9,... | collective-permute-start | bytes 1572872 | tf_op jit(solution)/shard_map/while/body/eval_jaxpr/ppermute | solution.py:12
  104.3 22.8 %collective-permute-start = (f32[1024,2,64]{0,2,1:T(8,128)S(1)}, f32[1024,2,64]{0,2,1:T(8,128)S(1)}, u32[]{:S(2)}, u32[]{:S(2)}) collective-permute-start(f32[1024,2,64]{0,2,1:T(8,128)S(1)} %get-tuple-element.565), channel_id=1, source_target_pairs={{0,4},{4,8},{8,12},{12,16},{16,20},{20,24},{24,28},{1,5},{5,9},{9,... | collective-permute-start | bytes 1572872 | tf_op jit(solution)/shard_map/while/body/eval_jaxpr/ppermute | solution.py:12
  127.1 12.0 %collective-permute-start = (f32[1024,2,64]{0,2,1:T(8,128)S(1)}, f32[1024,2,64]{0,2,1:T(8,128)S(1)}, u32[]{:S(2)}, u32[]{:S(2)}) collective-permute-start(f32[1024,2,64]{0,2,1:T(8,128)S(1)} %get-tuple-element.565), channel_id=1, source_target_pairs={{0,4},{4,8},{8,12},{12,16},{16,20},{20,24},{24,28},{1,5},{5,9},{9,... | collective-permute-start | bytes 1572872 | tf_op jit(solution)/shard_map/while/body/eval_jaxpr/ppermute | solution.py:12
  139.1 20.1 %collective-permute-start = (f32[1024,2,64]{0,2,1:T(8,128)S(1)}, f32[1024,2,64]{0,2,1:T(8,128)S(1)}, u32[]{:S(2)}, u32[]{:S(2)}) collective-permute-start(f32[1024,2,64]{0,2,1:T(8,128)S(1)} %get-tuple-element.565), channel_id=1, source_target_pairs={{0,4},{4,8},{8,12},{12,16},{16,20},{20,24},{24,28},{1,5},{5,9},{9,... | collective-permute-start | bytes 1572872 | tf_op jit(solution)/shard_map/while/body/eval_jaxpr/ppermute | solution.py:12
  159.2 11.2 %collective-permute-start = (f32[1024,2,64]{0,2,1:T(8,128)S(1)}, f32[1024,2,64]{0,2,1:T(8,128)S(1)}, u32[]{:S(2)}, u32[]{:S(2)}) collective-permute-start(f32[1024,2,64]{0,2,1:T(8,128)S(1)} %get-tuple-element.565), channel_id=1, source_target_pairs={{0,4},{4,8},{8,12},{12,16},{16,20},{20,24},{24,28},{1,5},{5,9},{9,... | collective-permute-start | bytes 1572872 | tf_op jit(solution)/shard_map/while/body/eval_jaxpr/ppermute | solution.py:12
  171.5 20.3 %collective-permute-start.1 = (bf16[1024,2,64]{0,2,1:T(8,128)(2,1)S(1)}, bf16[1024,2,64]{0,2,1:T(8,128)(2,1)S(1)}, u32[]{:S(2)}, u32[]{:S(2)}) collective-permute-start(bf16[1024,2,64]{0,2,1:T(8,128)(2,1)S(1)} %get-tuple-element.595), channel_id=1, source_target_pairs={{4,0},{8,4},{12,8},{16,12},{20,16},{24,20},{28,24},{5,1},{9,5},{13... | collective-permute-start | bytes 786440 | tf_op jit(solution)/shard_map/while/body/eval_jaxpr/ppermute | solution.py:12
  191.8 8.3 %collective-permute-start.1 = (bf16[1024,2,64]{0,2,1:T(8,128)(2,1)S(1)}, bf16[1024,2,64]{0,2,1:T(8,128)(2,1)S(1)}, u32[]{:S(2)}, u32[]{:S(2)}) collective-permute-start(bf16[1024,2,64]{0,2,1:T(8,128)(2,1)S(1)} %get-tuple-element.595), channel_id=1, source_target_pairs={{4,0},{8,4},{12,8},{16,12},{20,16},{24,20},{28,24},{5,1},{9,5},{13... | collective-permute-start | bytes 786440 | tf_op jit(solution)/shard_map/while/body/eval_jaxpr/ppermute | solution.py:12
  200.1 23.8 %collective-permute-start.1 = (bf16[1024,2,64]{0,2,1:T(8,128)(2,1)S(1)}, bf16[1024,2,64]{0,2,1:T(8,128)(2,1)S(1)}, u32[]{:S(2)}, u32[]{:S(2)}) collective-permute-start(bf16[1024,2,64]{0,2,1:T(8,128)(2,1)S(1)} %get-tuple-element.595), channel_id=1, source_target_pairs={{4,0},{8,4},{12,8},{16,12},{20,16},{24,20},{28,24},{5,1},{9,5},{13... | collective-permute-start | bytes 786440 | tf_op jit(solution)/shard_map/while/body/eval_jaxpr/ppermute | solution.py:12
  223.9 10.0 %collective-permute-start.1 = (bf16[1024,2,64]{0,2,1:T(8,128)(2,1)S(1)}, bf16[1024,2,64]{0,2,1:T(8,128)(2,1)S(1)}, u32[]{:S(2)}, u32[]{:S(2)}) collective-permute-start(bf16[1024,2,64]{0,2,1:T(8,128)(2,1)S(1)} %get-tuple-element.595), channel_id=1, source_target_pairs={{4,0},{8,4},{12,8},{16,12},{20,16},{24,20},{28,24},{5,1},{9,5},{13... | collective-permute-start | bytes 786440 | tf_op jit(solution)/shard_map/while/body/eval_jaxpr/ppermute | solution.py:12
  233.9 19.1 %collective-permute-start.1 = (bf16[1024,2,64]{0,2,1:T(8,128)(2,1)S(1)}, bf16[1024,2,64]{0,2,1:T(8,128)(2,1)S(1)}, u32[]{:S(2)}, u32[]{:S(2)}) collective-permute-start(bf16[1024,2,64]{0,2,1:T(8,128)(2,1)S(1)} %get-tuple-element.595), channel_id=1, source_target_pairs={{4,0},{8,4},{12,8},{16,12},{20,16},{24,20},{28,24},{5,1},{9,5},{13... | collective-permute-start | bytes 786440 | tf_op jit(solution)/shard_map/while/body/eval_jaxpr/ppermute | solution.py:12
  253.0 10.6 %collective-permute-start.1 = (bf16[1024,2,64]{0,2,1:T(8,128)(2,1)S(1)}, bf16[1024,2,64]{0,2,1:T(8,128)(2,1)S(1)}, u32[]{:S(2)}, u32[]{:S(2)}) collective-permute-start(bf16[1024,2,64]{0,2,1:T(8,128)(2,1)S(1)} %get-tuple-element.595), channel_id=1, source_target_pairs={{4,0},{8,4},{12,8},{16,12},{20,16},{24,20},{28,24},{5,1},{9,5},{13... | collective-permute-start | bytes 786440 | tf_op jit(solution)/shard_map/while/body/eval_jaxpr/ppermute | solution.py:12
  263.6 8.3 %collective-permute-start.1 = (bf16[1024,2,64]{0,2,1:T(8,128)(2,1)S(1)}, bf16[1024,2,64]{0,2,1:T(8,128)(2,1)S(1)}, u32[]{:S(2)}, u32[]{:S(2)}) collective-permute-start(bf16[1024,2,64]{0,2,1:T(8,128)(2,1)S(1)} %get-tuple-element.595), channel_id=1, source_target_pairs={{4,0},{8,4},{12,8},{16,12},{20,16},{24,20},{28,24},{5,1},{9,5},{13... | collective-permute-start | bytes 786440 | tf_op jit(solution)/shard_map/while/body/eval_jaxpr/ppermute | solution.py:12
  271.9 70.0 %collective-permute-start.1 = (bf16[1024,2,64]{0,2,1:T(8,128)(2,1)S(1)}, bf16[1024,2,64]{0,2,1:T(8,128)(2,1)S(1)}, u32[]{:S(2)}, u32[]{:S(2)}) collective-permute-start(bf16[1024,2,64]{0,2,1:T(8,128)(2,1)S(1)} %get-tuple-element.595), channel_id=1, source_target_pairs={{4,0},{8,4},{12,8},{16,12},{20,16},{24,20},{28,24},{5,1},{9,5},{13... | collective-permute-start | bytes 786440 | tf_op jit(solution)/shard_map/while/body/eval_jaxpr/ppermute | solution.py:12
  346.8 2.8 copy-start.1
  351.6 9.1 %collective-permute-start.1 = (bf16[1024,2,64]{0,2,1:T(8,128)(2,1)S(1)}, bf16[1024,2,64]{0,2,1:T(8,128)(2,1)S(1)}, u32[]{:S(2)}, u32[]{:S(2)}) collective-permute-start(bf16[1024,2,64]{0,2,1:T(8,128)(2,1)S(1)} %get-tuple-element.595), channel_id=1, source_target_pairs={{4,0},{8,4},{12,8},{16,12},{20,16},{24,20},{28,24},{5,1},{9,5},{13... | collective-permute-start | bytes 786440 | tf_op jit(solution)/shard_map/while/body/eval_jaxpr/ppermute | solution.py:12
  365.6 2.8 copy-start.1
where the time goes:
time: 375 us; the launch traced here: 374 us
  waiting for transfers between devices  244 us (65%)
  starting transfers between devices  79.8 us (21%)
  matrix products  33 us (9%)
  local copies, waits for them, and re-layouts  9.09 us (2%)
  other arithmetic  7.45 us (2%)
    ppermute x18, waiting for transfers between devices, shifted(): lax.ppermute(value, axis, [(source, source + steps) for source in range(i...  244 us
    ppermute x18, starting transfers between devices, shifted(): lax.ppermute(value, axis, [(source, source + steps) for source in range(i...  79.8 us
    dot_general x8, matrix products, complex_apply(): jnp.dot(real_part, merged, preferred_element_type=jnp.float32)  19.9 us
    dot_general x8, matrix products, complex_apply(): jnp.dot(imag_part, merged, preferred_element_type=jnp.float32)  13 us
  transfers between devices with their start and end apart: 18, of which 18 were waited for; matrix products, arithmetic and copies ran while one was open for 0% of the time, Pallas kernels for 0%

commit v1 on v0

v1 whole, which is shorter than its diff:
```python
import functools

import jax
import jax.numpy as jnp
from jax import lax
from jax.experimental import pallas as pl
from jax.experimental.pallas import tpu as pltpu
from jax.sharding import PartitionSpec as P

BATCHES = 8
BLOCK = 256
F32 = jnp.float32
BF16 = jnp.bfloat16
MESH = pl.DeviceIdType.MESH
PLAIN = (((1,), (0,)), ((), ()))
ACROSS = (((1,), (1,)), ((), ()))


def complex_rows(vectors, real_part, imag_part, dims):
    chunks, rows, modes = vectors.shape
    merged = vectors.reshape(chunks * rows, modes)
    split = (chunks, 2, rows // 2, modes)
    direct = lax.dot_general(merged, real_part, dims, preferred_element_type=F32).reshape(split)
    crossed = lax.dot_general(merged, imag_part, dims, preferred_element_type=F32).reshape(split)
    both = jnp.concatenate([direct[:, :1] - crossed[:, 1:], direct[:, 1:] + crossed[:, :1]], axis=1)
    return both.reshape(chunks, rows, modes)


def kernel(
    strips, src_hbm, pr_hbm, pi_hbm, out, src, pr, pi, fwd_r, fwd_i, bwd_r, bwd_i, last_trace, base,
    fin, fout, bin_, bout, load_sem, fsend, frecv, bsend, brecv,
):
    me = lax.axis_index("strip")
    batches, rows, modes = fin.shape
    is_first, is_last = me == 0, me == strips - 1
    after, before = jnp.minimum(me + 1, strips - 1), jnp.maximum(me - 1, 0)
    barrier = pltpu.get_barrier_semaphore()

    @pl.when(jnp.logical_not(is_first))
    def _():
        pl.semaphore_signal(barrier, inc=1, device_id={"strip": before}, device_id_type=MESH)

    @pl.when(jnp.logical_not(is_last))
    def _():
        pl.semaphore_signal(barrier, inc=1, device_id={"strip": after}, device_id_type=MESH)

    loads = [
        pltpu.make_async_copy(source.at[layer], target.at[layer], load_sem.at[3 * layer + which])
        for layer in range(2)
        for which, (source, target) in enumerate(((src_hbm, src), (pr_hbm, pr), (pi_hbm, pi)))
    ]
    for load in loads:
        load.start()

    def forward_copy(b):
        return pltpu.make_async_remote_copy(
            src_ref=fout.at[b], dst_ref=fin.at[b], send_sem=fsend.at[b], recv_sem=frecv.at[b],
            device_id={"strip": after}, device_id_type=MESH,
        )

    def backward_copy(b):
        return pltpu.make_async_remote_copy(
            src_ref=bout.at[b], dst_ref=bin_.at[b], send_sem=bsend.at[b], recv_sem=brecv.at[b],
            device_id={"strip": before}, device_id_type=MESH,
        )

    for load in loads[:3]:
        load.wait()
    trace = complex_rows(src[0], pr[0], pi[0], ACROSS)
    for load in loads[3:]:
        load.wait()
    summed = (src[1].astype(F32) + trace).astype(BF16)
    last_trace[...] = complex_rows(summed, pr[1], pi[1], ACROSS)

    inner = jnp.logical_not(jnp.logical_or(is_first, is_last))

    @pl.when(inner)
    def _():
        pl.semaphore_wait(barrier, 2)

    @pl.when(jnp.logical_not(inner))
    def _():
        pl.semaphore_wait(barrier, 1)

    def each(body):
        def step(b, carry):
            body(b)
            return carry

        lax.fori_loop(0, batches, step, 0)

    @pl.when(is_first)
    def _():
        @each
        def _(b):
            fout[b] = last_trace[b].astype(BF16)
            forward_copy(b).start()

    def product_rows(left_r, left_i, right_r, right_i):
        real = jnp.dot(left_r, right_r, preferred_element_type=F32) - jnp.dot(
            left_i, right_i, preferred_element_type=F32
        )
        imag = jnp.dot(left_r, right_i, preferred_element_type=F32) + jnp.dot(
            left_i, right_r, preferred_element_type=F32
        )
        return real, imag

    def build(target_r, target_i, compute):
        def step(i, carry):
            block = pl.ds(pl.multiple_of(i * BLOCK, BLOCK), BLOCK)
            real, imag = compute(block)
            target_r[:, block] = real.T.astype(BF16)
            target_i[:, block] = imag.T.astype(BF16)
            return carry

        lax.fori_loop(0, modes // BLOCK, step, 0)

    def forward_rows(block):
        return product_rows(pr[1, block, :], pi[1, block, :], pr[0], pi[0])

    def backward_rows(block):
        return product_rows(pr[0, block, :], pi[0, block, :], pr[1], pi[1])

    def turn_rows(block):
        real, imag = backward_rows(block)
        real, imag = product_rows(real.astype(BF16), imag.astype(BF16), pr[0], pi[0])
        return real + pr[0, block, :].astype(F32), imag + pi[0, block, :].astype(F32)

    early = me < strips // 2

    @pl.when(inner)
    def _():
        build(fwd_r, fwd_i, forward_rows)

    @pl.when(jnp.logical_and(inner, jnp.logical_not(early)))
    def _():
        build(bwd_r, bwd_i, backward_rows)

    @pl.when(inner)
    def _():
        @each
        def _(b):
            forward_copy(b).wait_recv()
            total = last_trace[b] + complex_rows(fin[b][None], fwd_r[...], fwd_i[...], PLAIN)[0]
            fout[b] = total.astype(BF16)
            forward_copy(b).start()
            last_trace[b] = total

    @pl.when(is_last)
    def _():
        build(bwd_r, bwd_i, turn_rows)
        known = src[0].astype(F32) + last_trace[...]
        base[...] = complex_rows(known.astype(BF16), pr[0], pi[0], ACROSS)

        @each
        def _(b):
            forward_copy(b).wait_recv()
            total = base[b] + complex_rows(fin[b][None], bwd_r[...], bwd_i[...], PLAIN)[0]
            bout[b] = total.astype(BF16)
            backward_copy(b).start()
            out[0, b] = total.astype(BF16)

        passed = complex_rows(fin[...], pr[0], pi[0], ACROSS).astype(BF16)
        field = last_trace[...] + complex_rows(passed, pr[1], pi[1], ACROSS)
        out[1] = field.astype(BF16)

    @pl.when(inner)
    def _():
        known = src[0].astype(F32) + fin[...].astype(F32) + last_trace[...]
        base[...] = complex_rows(known.astype(BF16), pr[0], pi[0], ACROSS)

    @pl.when(is_first)
    def _():
        known = src[0].astype(F32) + last_trace[...]
        base[...] = complex_rows(known.astype(BF16), pr[0], pi[0], ACROSS)

    @pl.when(jnp.logical_and(early, jnp.logical_not(is_last)))
    def _():
        build(bwd_r, bwd_i, backward_rows)

    @pl.when(jnp.logical_not(is_last))
    def _():
        @each
        def _(b):
            backward_copy(b).wait_recv()
            total = base[b] + complex_rows(bin_[b][None], bwd_r[...], bwd_i[...], PLAIN)[0]
            field = total.astype(BF16)
            out[0, b] = field

            @pl.when(jnp.logical_not(is_first))
            def _():
                bout[b] = field
                backward_copy(b).start()

        field = last_trace[...] + complex_rows(bin_[...], pr[1], pi[1], ACROSS)
        out[1] = field.astype(BF16)

        @each
        def _(b):
            forward_copy(b).wait_send()

    @pl.when(jnp.logical_not(is_first))
    def _():
        @each
        def _(b):
            backward_copy(b).wait_send()


def solution(mesh):
    strips = mesh.shape["strip"]

    def step(source, pivot_inverse_real, factor_imag):
        layers, modes, halves, columns = source.shape
        width = columns // BATCHES
        rows = halves * width
        chunked = (layers, BATCHES, rows, modes)
        placed = source.reshape(layers, modes, halves, BATCHES, width)
        placed = placed.transpose(0, 3, 2, 4, 1).reshape(chunked)
        anywhere = pl.BlockSpec(memory_space=pl.ANY)
        vectors = (BATCHES, rows, modes)
        square = (modes, modes)
        result = pl.pallas_call(
            functools.partial(kernel, strips),
            out_shape=jax.ShapeDtypeStruct(chunked, BF16),
            in_specs=[anywhere] * 3,
            out_specs=pl.BlockSpec(memory_space=pltpu.VMEM),
            scratch_shapes=[
                pltpu.VMEM(chunked, BF16),
                pltpu.VMEM((layers,) + square, BF16),
                pltpu.VMEM((layers,) + square, BF16),
            ]
            + [pltpu.VMEM(square, BF16)] * 4
            + [pltpu.VMEM(vectors, F32)] * 2
            + [pltpu.VMEM(vectors, BF16)] * 4
            + [pltpu.SemaphoreType.DMA((6,))]
            + [pltpu.SemaphoreType.DMA((BATCHES,))] * 4,
            compiler_params=pltpu.CompilerParams(
                collective_id=0, has_side_effects=True, vmem_limit_bytes=56 * 1024 * 1024
            ),
        )(placed, pivot_inverse_real, factor_imag)
        result = result.reshape(layers, BATCHES, halves, width, modes)
        return result.transpose(0, 4, 2, 1, 3).reshape(source.shape)

    return jax.shard_map(
        step,
        mesh=mesh,
        in_specs=(P("strip", None, None, "wave"), P("strip", "wave", None), P("strip", "wave", None)),
        out_specs=P("strip", None, None, "wave"),
        check_vma=False,
    )
```

time: 375 us -> 97.2 us (0.26)
  waiting for transfers between devices: 244 us -> 0 us
  Pallas kernels: 0 us -> 90.2 us
  starting transfers between devices: 79.8 us -> 0 us
  matrix products: 33 us -> 0 us
  other arithmetic: 7.45 us -> 0 us
    ppermute x18 -> x0, waiting for transfers between devices: 244 us -> none  [shifted(): lax.ppermute(value, axis, [(source, source + steps) for source in range(i...]
    pallas_call x0 -> x1, Pallas kernels: none -> 90.2 us  [step(): pl.pallas_call(functools.partial(kernel, strips), out_shape=jax.ShapeDtyp...]
    ppermute x18 -> x0, starting transfers between devices: 79.8 us -> none  [shifted(): lax.ppermute(value, axis, [(source, source + steps) for source in range(i...]
    dot_general x16 -> x0, matrix products: 33 us -> none  [the longest x8 19.9 us: complex_apply(): jnp.dot(real_part, merged, preferred_element_type=jnp.float32)]
    while x2 -> x0, local copies, waits for them, and re-layouts: 7.31 us -> none  [shards(): lax.fori_loop(0, strips + batches - 1, lambda moment, current: advance(mo...]
  transfers between devices with their start and end apart: 18 -> 0, of which waited for: 18 -> 0; matrix products, arithmetic and copies ran while one was open for 0% -> 0% of each run, Pallas kernels for 0% -> 0%
where the time goes in v1:
time: 97.2 us; the launch traced here: 97 us
  Pallas kernels  90.2 us (93%)
  local copies, waits for them, and re-layouts  6.8 us (7%)
    pallas_call x1, Pallas kernels, step(): pl.pallas_call(functools.partial(kernel, strips), out_shape=jax.ShapeDtyp...  90.2 us
    unnamed x1, local copies, waits for them, and re-layouts  2.45 us
    reshape x1, local copies, waits for them, and re-layouts, step(): return result.transpose(0, 4, 2, 1, 3).reshape(source.shape)  2 us

profile of v1, /device:TPU:0, one launch (start us, length us, event | category | flops | bytes accessed | tf_op | source)
XLA Modules:
  0.0 97.0 jit_solution(13092413198935046482)
XLA Ops:
  0.0 2.4 %copy.6 = bf16[2,1024,2,128]{1,3,2,0:T(8,128)(2,1)S(1)} copy(bf16[2,1024,2,128]{3,2,1,0:T(2,128)(2,1)} %param.3) | data formatting | bytes 2097152 | tf_op args[0]
  2.5 1.0 %copy.7 = bf16[2,8,2,16,1024]{4,3,2,1,0:T(8,128)(2,1)} copy(bf16[2,8,2,16,1024]{4,3,1,2,0:T(8,128)(2,1)S(1)} %bitcast.11) | data formatting | bytes 2097152 | tf_op jit(solution)/shard_map/transpose | solution.py:218
  3.5 90.2 %shard_map.37 = bf16[2,8,32,1024]{3,2,1,0:T(8,128)(2,1)} custom-call(bf16[2,8,32,1024]{3,2,1,0:T(8,128)(2,1)} %bitcast.8, bf16[2,1024,1024]{2,1,0:T(8,128)(2,1)} %pr_hbm.1, bf16[2,1024,1024]{2,1,0:T(8,128)(2,1)} %pi_hbm.1), custom_call_target="tpu_custom_call" | custom-call | tf_op jit(solution)/shard_map/pallas_call | solution.py:222
  93.7 1.3 %copy.8 = bf16[2,8,2,16,1024]{4,3,1,2,0:T(8,128)(2,1)S(1)} copy(bf16[2,8,2,16,1024]{4,3,2,1,0:T(8,128)(2,1)} %bitcast.9) | data formatting | bytes 2097152 | tf_op jit(solution)/shard_map/reshape | solution.py:241
  95.0 2.0 %copy.9 = bf16[2,1024,2,128]{3,2,1,0:T(2,128)(2,1)} copy(bf16[2,1024,2,128]{1,3,2,0:T(8,128)(2,1)S(1)} %bitcast.10) | data formatting | bytes 2097152 | tf_op jit(solution)/shard_map/reshape | solution.py:242

commit v2 on v1

--- a/solution.py
+++ b/solution.py
@@ -8,6 +8,7 @@
 from jax.sharding import PartitionSpec as P
 
 BATCHES = 8
+PIECES = 2
 BLOCK = 256
 F32 = jnp.float32
 BF16 = jnp.bfloat16
@@ -16,14 +17,17 @@
 ACROSS = (((1,), (1,)), ((), ()))
 
 
+def combine(direct, crossed):
+    return jnp.stack([direct[0] - crossed[1], direct[1] + crossed[0]])
+
+
 def complex_rows(vectors, real_part, imag_part, dims):
-    chunks, rows, modes = vectors.shape
-    merged = vectors.reshape(chunks * rows, modes)
-    split = (chunks, 2, rows // 2, modes)
-    direct = lax.dot_general(merged, real_part, dims, preferred_element_type=F32).reshape(split)
-    crossed = lax.dot_general(merged, imag_part, dims, preferred_element_type=F32).reshape(split)
-    both = jnp.concatenate([direct[:, :1] - crossed[:, 1:], direct[:, 1:] + crossed[:, :1]], axis=1)
-    return both.reshape(chunks, rows, modes)
+    halves, columns, modes = vectors.shape
+    merged = vectors.reshape(halves * columns, modes)
+    outcome = (halves, columns, real_part.shape[1 - dims[0][1][0]])
+    direct = lax.dot_general(merged, real_part, dims, preferred_element_type=F32).reshape(outcome)
+    crossed = lax.dot_general(merged, imag_part, dims, preferred_element_type=F32).reshape(outcome)
+    return combine(direct, crossed)
 
 
 def kernel(
@@ -31,7 +35,10 @@
     fin, fout, bin_, bout, load_sem, fsend, frecv, bsend, brecv,
 ):
     me = lax.axis_index("strip")
-    batches, rows, modes = fin.shape
+    halves, columns, modes = fin.shape
+    batches = BATCHES
+    width = columns // batches
+    depth = modes // PIECES
     is_first, is_last = me == 0, me == strips - 1
     after, before = jnp.minimum(me + 1, strips - 1), jnp.maximum(me - 1, 0)
     barrier = pltpu.get_barrier_semaphore()
@@ -52,17 +59,47 @@
     for load in loads:
         load.start()
 
-    def forward_copy(b):
+    def columns_of(b):
+        return pl.ds(pl.multiple_of(b * width, width), width)
+
+    def modes_of(piece):
+        return pl.ds(piece * depth, depth)
+
+    def forward_copy(b, piece):
+        part = (slice(None), columns_of(b), modes_of(piece))
         return pltpu.make_async_remote_copy(
-            src_ref=fout.at[b], dst_ref=fin.at[b], send_sem=fsend.at[b], recv_sem=frecv.at[b],
+            src_ref=fout.at[part], dst_ref=fin.at[part],
+            send_sem=fsend.at[b * PIECES + piece], recv_sem=frecv.at[b * PIECES + piece],
             device_id={"strip": after}, device_id_type=MESH,
         )
 
-    def backward_copy(b):
+    def backward_copy(b, piece):
+        part = (slice(None), columns_of(b), modes_of(piece))
         return pltpu.make_async_remote_copy(
-            src_ref=bout.at[b], dst_ref=bin_.at[b], send_sem=bsend.at[b], recv_sem=brecv.at[b],
+            src_ref=bout.at[part], dst_ref=bin_.at[part],
+            send_sem=bsend.at[b * PIECES + piece], recv_sem=brecv.at[b * PIECES + piece],
             device_id={"strip": before}, device_id_type=MESH,
         )
+
+    def pass_on(b, copy, arriving, known, real_part, imag_part, emit):
+        part = columns_of(b)
+        total = known[:, part, :]
+        for piece in range(PIECES - 1):
+            copy(b, piece).wait_recv()
+            total = total + complex_rows(
+                arriving[:, part, modes_of(piece)],
+                real_part[modes_of(piece), :], imag_part[modes_of(piece), :], PLAIN,
+            )
+        copy(b, PIECES - 1).wait_recv()
+        ending = modes_of(PIECES - 1)
+        vectors = arriving[:, part, ending]
+        for piece in range(PIECES):
+            lanes = modes_of(piece)
+            emit(
+                piece, (slice(None), part, lanes),
+                total[:, :, piece * depth : (piece + 1) * depth]
+                + complex_rows(vectors, real_part[ending, lanes], imag_part[ending, lanes], PLAIN),
+            )
 
     for load in loads[:3]:
         load.wait()
@@ -93,8 +130,10 @@
     def _():
         @each
         def _(b):
-            fout[b] = last_trace[b].astype(BF16)
-            forward_copy(b).start()
+            part = columns_of(b)
+            fout[:, part, :] = last_trace[:, part, :].astype(BF16)
+            for piece in range(PIECES):
+                forward_copy(b, piece).start()
 
     def product_rows(left_r, left_i, right_r, right_i):
         real = jnp.dot(left_r, right_r, preferred_element_type=F32) - jnp.dot(
@@ -140,11 +179,12 @@
     def _():
         @each
         def _(b):
-            forward_copy(b).wait_recv()
-            total = last_trace[b] + complex_rows(fin[b][None], fwd_r[...], fwd_i[...], PLAIN)[0]
-            fout[b] = total.astype(BF16)
-            forward_copy(b).start()
-            last_trace[b] = total
+            def emit(piece, part, total):
+                fout[part] = total.astype(BF16)
+                forward_copy(b, piece).start()
+                last_trace[part] = total
+
+            pass_on(b, forward_copy, fin, last_trace, fwd_r, fwd_i, emit)
 
     @pl.when(is_last)
     def _():
@@ -154,11 +194,13 @@
 
         @each
         def _(b):
-            forward_copy(b).wait_recv()
-            total = base[b] + complex_rows(fin[b][None], bwd_r[...], bwd_i[...], PLAIN)[0]
-            bout[b] = total.astype(BF16)
-            backward_copy(b).start()
-            out[0, b] = total.astype(BF16)
+            def emit(piece, part, total):
+                field = total.astype(BF16)
+                bout[part] = field
+                backward_copy(b, piece).start()
+                out[(0,) + part] = field
+
+            pass_on(b, forward_copy, fin, base, bwd_r, bwd_i, emit)
 
         passed = complex_rows(fin[...], pr[0], pi[0], ACROSS).astype(BF16)
         field = last_trace[...] + complex_rows(passed, pr[1], pi[1], ACROSS)
@@ -182,28 +224,32 @@
     def _():
         @each
         def _(b):
-            backward_copy(b).wait_recv()
-            total = base[b] + complex_rows(bin_[b][None], bwd_r[...], bwd_i[...], PLAIN)[0]
-            field = total.astype(BF16)
-            out[0, b] = field
-
-            @pl.when(jnp.logical_not(is_first))
-            def _():
-                bout[b] = field
-                backward_copy(b).start()
+            def emit(piece, part, total):
+                field = total.astype(BF16)
+
+                @pl.when(jnp.logical_not(is_first))
+                def _():
+                    bout[part] = field
+                    backward_copy(b, piece).start()
+
+                out[(0,) + part] = field
+
+            pass_on(b, backward_copy, bin_, base, bwd_r, bwd_i, emit)
 
         field = last_trace[...] + complex_rows(bin_[...], pr[1], pi[1], ACROSS)
         out[1] = field.astype(BF16)
 
         @each
         def _(b):
-            forward_copy(b).wait_send()
+            for piece in range(PIECES):
+                forward_copy(b, piece).wait_send()
 
     @pl.when(jnp.logical_not(is_first))
     def _():
         @each
         def _(b):
-            backward_copy(b).wait_send()
+            for piece in range(PIECES):
+                backward_copy(b, piece).wait_send()
 
 
 def solution(mesh):
@@ -211,13 +257,10 @@
 
     def step(source, pivot_inverse_real, factor_imag):
         layers, modes, halves, columns = source.shape
-        width = columns // BATCHES
-        rows = halves * width
-        chunked = (layers, BATCHES, rows, modes)
-        placed = source.reshape(layers, modes, halves, BATCHES, width)
-        placed = placed.transpose(0, 3, 2, 4, 1).reshape(chunked)
+        placed = source.transpose(0, 2, 3, 1)
         anywhere = pl.BlockSpec(memory_space=pl.ANY)
-        vectors = (BATCHES, rows, modes)
+        vectors = (halves, columns, modes)
+        chunked = (layers,) + vectors
         square = (modes, modes)
         result = pl.pallas_call(
             functools.partial(kernel, strips),
@@ -233,13 +276,12 @@
             + [pltpu.VMEM(vectors, F32)] * 2
             + [pltpu.VMEM(vectors, BF16)] * 4
             + [pltpu.SemaphoreType.DMA((6,))]
-            + [pltpu.SemaphoreType.DMA((BATCHES,))] * 4,
+            + [pltpu.SemaphoreType.DMA((BATCHES * PIECES,))] * 4,
             compiler_params=pltpu.CompilerParams(
                 collective_id=0, has_side_effects=True, vmem_limit_bytes=56 * 1024 * 1024
             ),
         )(placed, pivot_inverse_real, factor_imag)
-        result = result.reshape(layers, BATCHES, halves, width, modes)
-        return result.transpose(0, 4, 2, 1, 3).reshape(source.shape)
+        return result.transpose(0, 3, 1, 2)
 
     return jax.shard_map(
         step,

time: 97.2 us -> 94.9 us (0.976)
  Pallas kernels: 90.2 us -> 87.4 us
    reshape x2 -> x0, local copies, waits for them, and re-layouts: 3.3 us -> none  [the longest x1 2 us: step(): return result.transpose(0, 4, 2, 1, 3).reshape(source.shape)]
    pallas_call x1, Pallas kernels: 90.2 us -> 87.4 us  [step(): pl.pallas_call(functools.partial(kernel, strips), out_shape=jax.ShapeDtyp...]
    transpose x1, local copies, waits for them, and re-layouts: 1.05 us -> 3.67 us  [step(): return result.transpose(0, 3, 1, 2)]
    unnamed x1, local copies, waits for them, and re-layouts: 2.45 us -> 3.65 us
where the time goes in v2:
time: 94.9 us; the launch traced here: 94.7 us
  Pallas kernels  87.4 us (92%)
  local copies, waits for them, and re-layouts  7.32 us (8%)
    pallas_call x1, Pallas kernels, step(): pl.pallas_call(functools.partial(kernel, strips), out_shape=jax.ShapeDtyp...  87.4 us
    transpose x1, local copies, waits for them, and re-layouts, step(): return result.transpose(0, 3, 1, 2)  3.67 us
    unnamed x1, local copies, waits for them, and re-layouts  3.65 us

profile of v2, /device:TPU:0, one launch (start us, length us, event | category | flops | bytes accessed | tf_op | source)
XLA Modules:
  0.0 94.7 jit_solution(15301787223100187538)
XLA Ops:
  0.0 3.7 %copy.4 = bf16[2,1024,2,128]{1,3,2,0:T(8,128)(2,1)} copy(bf16[2,1024,2,128]{3,2,1,0:T(2,128)(2,1)} %param.3) | data formatting | bytes 2097152 | tf_op args[0]
  3.7 87.4 %shard_map.37 = bf16[2,2,128,1024]{3,2,1,0:T(8,128)(2,1)} custom-call(bf16[2,2,128,1024]{3,2,1,0:T(8,128)(2,1)} %bitcast.3, bf16[2,1024,1024]{2,1,0:T(8,128)(2,1)} %pr_hbm.1, bf16[2,1024,1024]{2,1,0:T(8,128)(2,1)} %pi_hbm.1), custom_call_target="tpu_custom_call" | custom-call | tf_op jit(solution)/shard_map/pallas_call | solution.py:265
  91.0 3.7 %copy.5 = bf16[2,1024,2,128]{3,2,1,0:T(2,128)(2,1)} copy(bf16[2,1024,2,128]{1,3,2,0:T(8,128)(2,1)} %bitcast.2) | data formatting | bytes 2097152 | tf_op jit(solution)/shard_map/transpose | solution.py:284

commit v3 on v2

--- a/solution.py
+++ b/solution.py
@@ -9,6 +9,7 @@
 
 BATCHES = 8
 PIECES = 2
+GROUP = 2
 BLOCK = 256
 F32 = jnp.float32
 BF16 = jnp.bfloat16
@@ -167,7 +168,30 @@
 
     early = me < strips // 2
 
-    @pl.when(inner)
+    second = jnp.logical_and(inner, me == 1)
+    later = jnp.logical_and(inner, me != 1)
+
+    @pl.when(second)
+    def _():
+        def direct(g, carry):
+            for b in range(GROUP):
+                for piece in range(PIECES):
+                    forward_copy(g * GROUP + b, piece).wait_recv()
+            part = pl.ds(pl.multiple_of(g * (GROUP * width), width), GROUP * width)
+            summed = (src[0, :, part, :].astype(F32) + fin[:, part, :].astype(F32)).astype(BF16)
+            trace = complex_rows(summed, pr[0], pi[0], ACROSS)
+            summed = (src[1, :, part, :].astype(F32) + trace).astype(BF16)
+            trace = complex_rows(summed, pr[1], pi[1], ACROSS)
+            fout[:, part, :] = trace.astype(BF16)
+            for b in range(GROUP):
+                for piece in range(PIECES):
+                    forward_copy(g * GROUP + b, piece).start()
+            last_trace[:, part, :] = trace
+            return carry
+
+        lax.fori_loop(0, batches // GROUP, direct, 0)
+
+    @pl.when(later)
     def _():
         build(fwd_r, fwd_i, forward_rows)
 
@@ -175,7 +199,7 @@
     def _():
         build(bwd_r, bwd_i, backward_rows)
 
-    @pl.when(inner)
+    @pl.when(later)
     def _():
         @each
         def _(b):

time: 94.9 us -> 92.9 us (0.979)
  Pallas kernels: 87.4 us -> 85.3 us
    pallas_call x1, Pallas kernels: 87.4 us -> 85.3 us  [step(): pl.pallas_call(functools.partial(kernel, strips), out_shape=jax.ShapeDtyp...]
where the time goes in v3:
time: 92.9 us; the launch traced here: 92.7 us
  Pallas kernels  85.3 us (92%)
  local copies, waits for them, and re-layouts  7.32 us (8%)
    pallas_call x1, Pallas kernels, step(): pl.pallas_call(functools.partial(kernel, strips), out_shape=jax.ShapeDtyp...  85.3 us
    transpose x1, local copies, waits for them, and re-layouts, step(): return result.transpose(0, 3, 1, 2)  3.67 us
    unnamed x1, local copies, waits for them, and re-layouts  3.65 us

profile of v3, /device:TPU:0, one launch (start us, length us, event | category | flops | bytes accessed | tf_op | source)
XLA Modules:
  0.0 92.7 jit_solution(15679041473967470561)
XLA Ops:
  0.0 3.7 %copy.4 = bf16[2,1024,2,128]{1,3,2,0:T(8,128)(2,1)} copy(bf16[2,1024,2,128]{3,2,1,0:T(2,128)(2,1)} %param.3) | data formatting | bytes 2097152 | tf_op args[0]
  3.7 85.3 %shard_map.37 = bf16[2,2,128,1024]{3,2,1,0:T(8,128)(2,1)} custom-call(bf16[2,2,128,1024]{3,2,1,0:T(8,128)(2,1)} %bitcast.3, bf16[2,1024,1024]{2,1,0:T(8,128)(2,1)} %pr_hbm.1, bf16[2,1024,1024]{2,1,0:T(8,128)(2,1)} %pi_hbm.1), custom_call_target="tpu_custom_call" | custom-call | tf_op jit(solution)/shard_map/pallas_call | solution.py:289
  89.0 3.7 %copy.5 = bf16[2,1024,2,128]{3,2,1,0:T(2,128)(2,1)} copy(bf16[2,1024,2,128]{1,3,2,0:T(8,128)(2,1)} %bitcast.2) | data formatting | bytes 2097152 | tf_op jit(solution)/shard_map/transpose | solution.py:308

commit v4 on v3

--- a/solution.py
+++ b/solution.py
@@ -166,7 +166,7 @@
         real, imag = product_rows(real.astype(BF16), imag.astype(BF16), pr[0], pi[0])
         return real + pr[0, block, :].astype(F32), imag + pi[0, block, :].astype(F32)
 
-    early = me < strips // 2
+    early = me < strips - 3
 
     second = jnp.logical_and(inner, me == 1)
     later = jnp.logical_and(inner, me != 1)

time: 92.9 us -> 91.2 us (0.982)
  Pallas kernels: 85.3 us -> 83.6 us
    pallas_call x1, Pallas kernels: 85.3 us -> 83.6 us  [step(): pl.pallas_call(functools.partial(kernel, strips), out_shape=jax.ShapeDtyp...]
where the time goes in v4:
time: 91.2 us; the launch traced here: 91 us
  Pallas kernels  83.6 us (92%)
  local copies, waits for them, and re-layouts  7.32 us (8%)
    pallas_call x1, Pallas kernels, step(): pl.pallas_call(functools.partial(kernel, strips), out_shape=jax.ShapeDtyp...  83.6 us
    transpose x1, local copies, waits for them, and re-layouts, step(): return result.transpose(0, 3, 1, 2)  3.67 us
    unnamed x1, local copies, waits for them, and re-layouts  3.65 us

profile of v4, /device:TPU:0, one launch (start us, length us, event | category | flops | bytes accessed | tf_op | source)
XLA Modules:
  0.0 91.0 jit_solution(17125869171602666593)
XLA Ops:
  0.0 3.7 %copy.4 = bf16[2,1024,2,128]{1,3,2,0:T(8,128)(2,1)} copy(bf16[2,1024,2,128]{3,2,1,0:T(2,128)(2,1)} %param.3) | data formatting | bytes 2097152 | tf_op args[0]
  3.7 83.6 %shard_map.37 = bf16[2,2,128,1024]{3,2,1,0:T(8,128)(2,1)} custom-call(bf16[2,2,128,1024]{3,2,1,0:T(8,128)(2,1)} %bitcast.3, bf16[2,1024,1024]{2,1,0:T(8,128)(2,1)} %pr_hbm.1, bf16[2,1024,1024]{2,1,0:T(8,128)(2,1)} %pi_hbm.1), custom_call_target="tpu_custom_call" | custom-call | tf_op jit(solution)/shard_map/pallas_call | solution.py:289
  87.3 3.7 %copy.5 = bf16[2,1024,2,128]{3,2,1,0:T(2,128)(2,1)} copy(bf16[2,1024,2,128]{1,3,2,0:T(8,128)(2,1)} %bitcast.2) | data formatting | bytes 2097152 | tf_op jit(solution)/shard_map/transpose | solution.py:308

commit v5 on v4

--- a/solution.py
+++ b/solution.py
@@ -168,8 +168,8 @@
 
     early = me < strips - 3
 
-    second = jnp.logical_and(inner, me == 1)
-    later = jnp.logical_and(inner, me != 1)
+    second = jnp.logical_and(inner, me <= 2)
+    later = jnp.logical_and(inner, me > 2)
 
     @pl.when(second)
     def _():

time: 91.2 us -> 93.5 us (1.025)
  Pallas kernels: 83.6 us -> 85.9 us
    pallas_call x1, Pallas kernels: 83.6 us -> 85.9 us  [step(): pl.pallas_call(functools.partial(kernel, strips), out_shape=jax.ShapeDtyp...]
where the time goes in v5:
time: 93.5 us; the launch traced here: 93.2 us
  Pallas kernels  85.9 us (92%)
  local copies, waits for them, and re-layouts  7.32 us (8%)
    pallas_call x1, Pallas kernels, step(): pl.pallas_call(functools.partial(kernel, strips), out_shape=jax.ShapeDtyp...  85.9 us
    transpose x1, local copies, waits for them, and re-layouts, step(): return result.transpose(0, 3, 1, 2)  3.67 us
    unnamed x1, local copies, waits for them, and re-layouts  3.65 us

profile of v5, /device:TPU:0, one launch (start us, length us, event | category | flops | bytes accessed | tf_op | source)
XLA Modules:
  0.0 93.2 jit_solution(8001376490152279156)
XLA Ops:
  0.0 3.7 %copy.4 = bf16[2,1024,2,128]{1,3,2,0:T(8,128)(2,1)} copy(bf16[2,1024,2,128]{3,2,1,0:T(2,128)(2,1)} %param.3) | data formatting | bytes 2097152 | tf_op args[0]
  3.7 85.9 %shard_map.37 = bf16[2,2,128,1024]{3,2,1,0:T(8,128)(2,1)} custom-call(bf16[2,2,128,1024]{3,2,1,0:T(8,128)(2,1)} %bitcast.3, bf16[2,1024,1024]{2,1,0:T(8,128)(2,1)} %pr_hbm.1, bf16[2,1024,1024]{2,1,0:T(8,128)(2,1)} %pi_hbm.1), custom_call_target="tpu_custom_call" | custom-call | tf_op jit(solution)/shard_map/pallas_call | solution.py:289
  89.6 3.7 %copy.5 = bf16[2,1024,2,128]{3,2,1,0:T(2,128)(2,1)} copy(bf16[2,1024,2,128]{1,3,2,0:T(8,128)(2,1)} %bitcast.2) | data formatting | bytes 2097152 | tf_op jit(solution)/shard_map/transpose | solution.py:308
